TPU v7x, 512 devices: a whole 4x4x16 slice. The times are simulated.
512 devices in a mesh: dp: 32 (over z, core), seq: 16 (over y, x).
Axes of the slice: x: 4, y: 4, z: 16, core: 2. Of those that a mesh axis runs over, the one named last changes fastest.
Arguments:
- tokens: bfloat16 [65536, 1280], P(('dp', 'seq')), parts along dimension 0, may hold values from -6 to 6
- segment_ids: int32 [65536], P('dp'), parts along dimension 0, may hold values from 0 to 31, as said below
- w_qkv: bfloat16 [1280, 3840], P(None, 'seq')
- w_out: bfloat16 [1280, 1280], P('seq'), may hold values from -0.15625 to 0.15625
- w_merge: bfloat16 [5120, 4096], P(None, 'seq'), may hold values from -0.078125 to 0.078125
- gain_attn: float32 [1280], replicated, may hold values from 0.1 to 1.9
- gain_merge: float32 [1280], replicated, may hold values from 0.1 to 1.9
Outputs:
- merged_out: bfloat16 [16384, 4096], P(('dp', 'seq')), parts along dimension 0
There are 32 independent parts, one for each index of `dp`. A program takes and returns all parts, laid end to end along the dimension named above; an argument that names none is the same for every part. Nothing has to cross between parts.
Inputs may be any that keep to these rules, and one draw needn't show every extreme that they name: `segment_ids`: Non-decreasing along the packed tokens, starting at 0, rising by 0 or 1 from one token to the next, and equal within every aligned group of 4 tokens (an image's 2x2 patch blocks are stored together). There are exactly 32 images.
All inputs are finite; a program needn't handle non-finite values.
Results may differ from a plain program's by a relative error of at most 0.011.
Values may be sent and summed in bfloat16 or wider, within the bound.
No kernel may reach another device: no remote copies, remote signals or barrier semaphores. Data moves between devices by JAX's collectives and lax.ppermute only.
A program may use at most 64 MiB of HBM per device.

v0:
```python
import jax
import jax.numpy as jnp
from jax import lax
from jax.sharding import Mesh
from jax.sharding import PartitionSpec as P

D = 1280
HEADS = 16
HEAD_DIM = 80
SEQ = ("seq_0", "seq_1")
DP_SEQ = ("dp", "seq_0", "seq_1")


def gathered_by_axis(value, axes, dim):
    for axis in reversed(axes):
        value = lax.all_gather(value, axis, axis=dim, tiled=True)
    return value


def layer_norm(vector, scale_gain):
    average = jnp.mean(vector, axis=-1, keepdims=True)
    centred = vector - average
    spread_sq = jnp.mean(centred * centred, axis=-1, keepdims=True)
    return centred * lax.rsqrt(spread_sq + 1e-06) * scale_gain


def per_device(tokens, segment_ids, w_qkv, w_out, w_merge, gain_attn, gain_merge):
    group_size = lax.axis_size(SEQ)
    tok_local = tokens.shape[0]
    all_tokens = tok_local * group_size
    local_heads = HEADS // group_size
    residual = tokens.astype(jnp.float32)
    normed = layer_norm(residual, gain_attn).astype(jnp.bfloat16)
    qkv_rows = jnp.dot(
        lax.all_gather(normed, SEQ, axis=0, tiled=True), w_qkv, preferred_element_type=jnp.float32
    ).astype(jnp.bfloat16)
    qkv = qkv_rows.reshape(all_tokens, local_heads, 3, HEAD_DIM)
    key_rows = qkv[:, :, 1, :]
    value_rows = qkv[:, :, 2, :]
    block_rows = min(512, all_tokens)
    block_count = all_tokens // block_rows
    scale_factor = HEAD_DIM ** (-0.5)

    def masked_scores(queries, query_ids, key_part, key_ids):
        scores = (
            jnp.einsum("qhd,khd->hqk", queries, key_part, preferred_element_type=jnp.float32)
            * scale_factor
        )
        same_image = (query_ids[:, None] == key_ids[None, :])[None, :, :]
        return (jnp.where(same_image, scores, -jnp.inf), same_image)

    def query_block(block_index):
        query_start = block_index * block_rows
        queries = lax.dynamic_slice_in_dim(qkv, query_start, block_rows, 0)[:, :, 0, :]
        query_ids = lax.dynamic_slice_in_dim(segment_ids, query_start, block_rows, 0)
        scores, same_image = masked_scores(queries, query_ids, key_rows, segment_ids)
        row_max = jnp.max(scores, axis=-1, keepdims=True)
        expo = jnp.where(same_image, jnp.exp(scores - row_max), 0.0)
        row_sum = jnp.sum(expo, axis=-1)
        probs = expo.astype(jnp.bfloat16)
        summed = jnp.einsum("hqk,khd->qhd", probs, value_rows, preferred_element_type=jnp.float32)
        result = summed / row_sum.T[:, :, None]
        return result.astype(jnp.bfloat16).reshape(block_rows, local_heads * HEAD_DIM)

    attended = lax.map(query_block, jnp.arange(block_count, dtype=jnp.int32)).reshape(
        all_tokens, local_heads * HEAD_DIM
    )
    back = lax.all_to_all(attended, SEQ, split_axis=0, concat_axis=1, tiled=True)
    projected_attn = jnp.dot(
        back, gathered_by_axis(w_out, SEQ, 0), preferred_element_type=jnp.float32
    )
    hidden = residual + projected_attn
    normed_two = layer_norm(hidden, gain_merge).astype(jnp.bfloat16)
    merged = normed_two.reshape(tok_local // 4, 4 * D)
    column_block = jnp.dot(
        lax.all_gather(merged, SEQ, axis=0, tiled=True), w_merge, preferred_element_type=jnp.float32
    ).astype(jnp.bfloat16)
    return lax.all_to_all(column_block, SEQ, split_axis=0, concat_axis=1, tiled=True)


def solution(mesh):
    torus = Mesh(mesh.devices.reshape(mesh.shape["dp"], 4, 4), ("dp", "seq_0", "seq_1"))
    in_specs = (P(DP_SEQ, None), P("dp"), P(None, SEQ), P(SEQ, None), P(None, SEQ), P(), P())
    out_specs = P(DP_SEQ, None)
    return jax.shard_map(
        per_device, mesh=torus, in_specs=in_specs, out_specs=out_specs, check_vma=False
    )
```

profile of v0, /device:TPU:32, one launch (start us, length us, event | category | flops | bytes accessed | tf_op | source)
XLA Modules:
  0.0 241.4 jit_solution(16823086100214955920)
XLA Ops:
  6.5 1.2 convert_reduce_fusion
  7.8 1.2 fusion.29
  9.0 1.9 fusion.31
  10.9 0.0 all-gather.4.cloned.1.call-update
  11.0 0.0 all-gather.6.cloned.1.call-start
  11.0 16.2 %all_gather.13 = bf16[320,1280]{1,0:T(8,128)(2,1)} all-gather(bf16[80,1280]{1,0:T(8,128)(2,1)} %param.12), channel_id=1, replica_groups=mesh['dp'=32,'seq_0'=4,'seq_1'=4] {'seq_1'}, dimensions={0}, use_global_device_ids=true | all-gather | bytes 1024000 | tf_op jit(solution)/shard_map/all_gather | solution.py:16
  27.2 0.0 all-gather.6.cloned.1.call-update
  27.3 0.0 copy-start.3
  27.3 59.5 %all-gather.4.cloned.1.call-done = bf16[2048,1280]{1,0:T(8,128)(2,1)} async-done(((bf16[128,1280]{1,0:T(8,128)(2,1)}), bf16[2048,1280]{1,0:T(8,128)(2,1)}) %all-gather.4.cloned.1.call-update) | async-done | bytes 5242896 | tf_op jit(solution)/shard_map/all_gather | solution.py:35
  86.8 4.2 %convolution_convert_fusion = bf16[2048,240]{0,1:T(8,128)(2,1)S(1)} fusion(bf16[2048,1280]{1,0:T(8,128)(2,1)} %all-gather.4.cloned.1.call-done, bf16[1280,240]{0,1:T(8,128)(2,1)} %param.11), kind=kOutput, calls=%fused_computation.19 | convolution fusion | flops 1258782720 | bytes 6840320 | tf_op jit(solution)/shard_map/dot_general | solution.py:34
  91.0 0.9 slice_bitcast_fusion
  91.8 0.2 copy-done.2
  92.0 25.1 %while.10 = (s32[]{:T(128)}, bf16[4,512,80]{1,2,0:T(8,128)(2,1)}, s32[4]{0:T(128)S(1)}, s32[2048]{0:T(1024)S(1)}, bf16[2048,1,3,80]{0,3,2,1:T(8,128)(2,1)}, /*in...) while((s32[]{:T(128)}, bf16[4,512,80]{1,2,0:T(8,128)(2,1)}, ...), condition=%wide.region_5.6_spmd, body=%wide.region_2.5_spmd.sunk | while | flops 352402432 | bytes 13447855 | solution.py:65
  92.0 0.6 dynamic_slice.12
  93.2 0.1 dynamic_slice.13
  93.3 1.9 fusion.46
  95.2 1.2 fusion.47
  96.4 1.9 fusion.48
  98.3 0.6 dynamic_slice.12
  99.5 0.1 dynamic_slice.13
  99.5 1.9 fusion.46
  101.4 1.2 fusion.47
  102.7 1.9 fusion.48
  104.5 0.6 dynamic_slice.12
  105.7 0.1 dynamic_slice.13
  105.8 1.9 fusion.46
  107.7 1.2 fusion.47
  109.0 1.9 fusion.48
  110.9 0.6 dynamic_slice.12
  112.0 0.1 dynamic_slice.13
  112.1 1.9 fusion.46
  114.0 1.2 fusion.47
  115.3 1.9 fusion.48
  117.1 1.2 copy.15
  118.4 0.8 all_to_all.28
  119.2 1.8 copy.16
  121.0 5.3 %all-to-all-start = ((bf16[16,128,80]{1,2,0:T(8,128)(2,1)}), bf16[16,128,80]{1,2,0:T(8,128)(2,1)S(1)}, u32[]{:S(2)}, u32[]{:S(2)}) async-start(bf16[16,128,80]{1,2,0:T(8,128)(2,1)} %copy.16), calls=%async_computation | async-start | bytes 655360 | tf_op jit(solution)/shard_map/all_to_all | solution.py:68
  126.2 0.0 all-gather.8.cloned.1.call-start
  126.3 14.2 %all-gather.6.cloned.1.call-done = bf16[1280,1280]{1,0:T(8,128)(2,1)} async-done(((bf16[320,1280]{1,0:T(8,128)(2,1)}), bf16[1280,1280]{1,0:T(8,128)(2,1)}) %all-gather.6.cloned.1.call-update) | async-done | bytes 3276816 | tf_op jit(solution)/shard_map/all_gather | solution.py:16
  140.5 2.6 %fusion.32 = (f32[128]{0:T(128)S(1)}, f32[128,1280]{1,0:T(8,128)S(1)}) fusion(bf16[128,1280]{0,1:T(8,128)(2,1)S(1)} %bitcast.64, bf16[1280,1280]{1,0:T(8,128)(2,1)} %all-gather.6.cloned.1.call-done, bf16[128,1280]{1,0:T(8,128)(2,1)S(1)} %copy-done.1), kind=kOutput, calls=%fused_computation.37 | convolution fusion | flops 419921792 | bytes 4588032 | tf_op jit(solution)/shard_map/dot_general | solution.py:69
  143.2 0.2 multiply_reduce_fusion
  143.4 0.2 multiply_convert_fusion
  143.6 0.9 reshape.77
  144.5 0.0 all-gather.8.cloned.1.call-update
  144.5 71.9 %all-gather.8.cloned.1.call-done = bf16[512,5120]{1,0:T(8,128)(2,1)} async-done(((bf16[32,5120]{1,0:T(8,128)(2,1)}), bf16[512,5120]{1,0:T(8,128)(2,1)}) %all-gather.8.cloned.1.call-update) | async-done | bytes 5242896 | tf_op jit(solution)/shard_map/all_gather | solution.py:76
  216.4 4.0 %convolution_convert_fusion.1 = bf16[512,256]{1,0:T(8,128)(2,1)S(1)} fusion(bf16[512,5120]{1,0:T(8,128)(2,1)} %all-gather.8.cloned.1.call-done, bf16[5120,256]{1,0:T(8,128)(2,1)S(1)} %copy-done), kind=kOutput, calls=%fused_computation.21 | convolution fusion | flops 1342308352 | bytes 8126464 | tf_op jit(solution)/shard_map/dot_general | solution.py:75
  220.4 13.7 %all_to_all.38 = bf16[16,32,256]{2,1,0:T(8,128)(2,1)S(1)} all-to-all(bf16[16,32,256]{2,1,0:T(8,128)(2,1)S(1)} %bitcast.68), channel_id=1, replica_groups=mesh['dp'=32,'seq_0'=4,'seq_1'=4] {'seq_0','seq_1'}, dimensions={0} | all-to-all | bytes 524288 | tf_op jit(solution)/shard_map/all_to_all | solution.py:78
  234.2 0.7 copy.18
  (16 shorter events, 0.1 us)
Async XLA Ops:
  6.5 209.9 %copy-start = (bf16[5120,256]{1,0:T(8,128)(2,1)S(1)}, bf16[5120,256]{1,0:T(8,128)(2,1)}, u32[]{:S(2)}) copy-start(bf16[5120,256]{1,0:T(8,128)(2,1)} %param.13) | copy-start | bytes 7864324
  6.5 80.2 %all-gather.4.cloned.1.call-start = ((), (), s32[]{:S(2)}) async-start(), calls=%async_computation.2 | async-start | bytes 5570560 | tf_op jit(solution)/shard_map/all_gather | solution.py:35
  11.0 129.5 %all-gather.6.cloned.1.call-start = ((), (), s32[]{:S(2)}) async-start(), calls=%async_computation.3 | async-start | bytes 4096000 | tf_op jit(solution)/shard_map/all_gather | solution.py:16
  27.3 64.8 %copy-start.3 = (s32[2048]{0:T(1024)S(1)}, s32[2048]{0:T(1024)}, u32[]{:S(2)}) copy-start(s32[2048]{0:T(1024)} %param.10) | copy-start | bytes 24580
  90.9 1.1 copy-start.2
  92.0 48.5 %copy-start.1 = (bf16[128,1280]{1,0:T(8,128)(2,1)S(1)}, bf16[128,1280]{1,0:T(8,128)(2,1)}, u32[]{:S(2)}) copy-start(bf16[128,1280]{1,0:T(8,128)(2,1)} %param.9) | copy-start | bytes 983044
  117.1 26.3 %copy-start.4 = (f32[1280]{0:T(1024)S(1)}, f32[1280]{0:T(1024)}, u32[]{:S(2)}) copy-start(f32[1280]{0:T(1024)} %param.15) | copy-start | bytes 15364
  121.0 19.5 %all-to-all-start = ((bf16[16,128,80]{1,2,0:T(8,128)(2,1)}), bf16[16,128,80]{1,2,0:T(8,128)(2,1)S(1)}, u32[]{:S(2)}, u32[]{:S(2)}) async-start(bf16[16,128,80]{1,2,0:T(8,128)(2,1)} %copy.16), calls=%async_computation | async-start | bytes 655360 | tf_op jit(solution)/shard_map/all_to_all | solution.py:68
  126.2 90.2 %all-gather.8.cloned.1.call-start = ((), (), s32[]{:S(2)}) async-start(), calls=%async_computation.4 | async-start | bytes 5570560 | tf_op jit(solution)/shard_map/all_gather | solution.py:76
Sparse Core Ops, SparseCore 0:
  11.1 75.6 all-gather.3
  88.9 51.5 all-gather.5
  144.6 71.7 all-gather.7
where the time goes:
time: 242 us; the launch traced here: 241 us
  waiting for transfers between devices  146 us (60%)
  blocking collectives  30 us (12%)
  matrix products  25.9 us (11%)
  between operations  13.2 us (5%)
  other arithmetic  9.78 us (4%)
  local copies, waits for them, and re-layouts  9.27 us (4%)
  starting transfers between devices  5.34 us (2%)
    all_gather x1, waiting for transfers between devices, per_device(): lax.all_gather(merged, SEQ, axis=0, tiled=True)  71.9 us
    all_gather x1, waiting for transfers between devices, per_device(): lax.all_gather(normed, SEQ, axis=0, tiled=True)  59.5 us
    all_gather x1, blocking collectives, gathered_by_axis(): value = lax.all_gather(value, axis, axis=dim, tiled=True)  16.2 us
    all_gather x1, waiting for transfers between devices, gathered_by_axis(): value = lax.all_gather(value, axis, axis=dim, tiled=True)  14.2 us
    all_to_all x1, blocking collectives, per_device(): lax.all_to_all(column_block, SEQ, split_axis=0, concat_axis=1, tiled=True)  13.7 us
    dot_general x4, matrix products, masked_scores(): jnp.einsum('qhd,khd->hqk', queries, key_part, preferred_element_type=jnp....  7.64 us
    dot_general x4, matrix products, query_block(): jnp.einsum('hqk,khd->qhd', probs, value_rows, preferred_element_type=jnp....  7.46 us
    all_to_all x1, starting transfers between devices, per_device(): lax.all_to_all(attended, SEQ, split_axis=0, concat_axis=1, tiled=True)  5.25 us
  transfers between devices with their start and end apart: 4, of which 3 were waited for; matrix products, arithmetic and copies ran while one was open for 13% of the time, Pallas kernels for 0%

commit v1 on v0

--- a/solution.py
+++ b/solution.py
@@ -32,7 +32,17 @@
     residual = tokens.astype(jnp.float32)
     normed = layer_norm(residual, gain_attn).astype(jnp.bfloat16)
     qkv_rows = jnp.dot(
-        lax.all_gather(normed, SEQ, axis=0, tiled=True), w_qkv, preferred_element_type=jnp.float32
+        jnp.concatenate(
+            lax.all_to_all(
+                jnp.stack([normed for _ in range(lax.axis_size(SEQ))], 0),
+                axis_name=SEQ,
+                split_axis=0,
+                concat_axis=0,
+            ),
+            0,
+        ),
+        w_qkv,
+        preferred_element_type=jnp.float32,
     ).astype(jnp.bfloat16)
     qkv = qkv_rows.reshape(all_tokens, local_heads, 3, HEAD_DIM)
     key_rows = qkv[:, :, 1, :]

time: 242 us -> 264 us (1.091)
  blocking collectives: 30 us -> 102 us
  waiting for transfers between devices: 146 us -> 86.7 us
  starting transfers between devices: 5.34 us -> 12.5 us
  local copies, waits for them, and re-layouts: 9.27 us -> 12.1 us
    all_gather x1, blocking collectives: 16.2 us -> 87.8 us  [gathered_by_axis(): value = lax.all_gather(value, axis, axis=dim, tiled=True)]
    all_gather x1 -> x0, waiting for transfers between devices: 59.5 us -> none  [per_device(): lax.all_gather(normed, SEQ, axis=0, tiled=True)]
    all_to_all x0 -> x1, starting transfers between devices: none -> 7.21 us  [per_device(): lax.all_to_all(jnp.stack([normed for _ in range(lax.axis_size(SEQ))], 0),...]
    another operation x0 -> x1, local copies, waits for them, and re-layouts: none -> 2.84 us  [per_device(): jnp.stack([normed for _ in range(lax.axis_size(SEQ))], 0)]
  transfers between devices with their start and end apart: 4 -> 4, of which waited for: 3 -> 2; matrix products, arithmetic and copies ran while one was open for 13% -> 12% of each run, Pallas kernels for 0% -> 0%
where the time goes in v1:
time: 264 us
  blocking collectives  102 us (39%)
  waiting for transfers between devices  86.7 us (33%)
  matrix products  25.9 us (10%)
  between operations  13.5 us (5%)
  starting transfers between devices  12.5 us (5%)
  local copies, waits for them, and re-layouts  12.1 us (5%)
  other arithmetic  9.05 us (3%)
    all_gather x1, blocking collectives, gathered_by_axis(): value = lax.all_gather(value, axis, axis=dim, tiled=True)  87.8 us
    all_gather x1, waiting for transfers between devices, per_device(): lax.all_gather(merged, SEQ, axis=0, tiled=True)  71.9 us
    all_gather x1, waiting for transfers between devices, gathered_by_axis(): value = lax.all_gather(value, axis, axis=dim, tiled=True)  14.7 us
    all_to_all x1, blocking collectives, per_device(): lax.all_to_all(column_block, SEQ, split_axis=0, concat_axis=1, tiled=True)  13.7 us
    dot_general x4, matrix products, masked_scores(): jnp.einsum('qhd,khd->hqk', queries, key_part, preferred_element_type=jnp....  7.64 us
    dot_general x4, matrix products, query_block(): jnp.einsum('hqk,khd->qhd', probs, value_rows, preferred_element_type=jnp....  7.48 us
    all_to_all x1, starting transfers between devices, per_device(): lax.all_to_all(jnp.stack([normed for _ in range(lax.axis_size(SEQ))], 0),...  7.21 us
  transfers between devices with their start and end apart: 4, of which 2 were waited for; matrix products, arithmetic and copies ran while one was open for 12% of the time, Pallas kernels for 0%

profile of v1, /device:TPU:32, one launch (start us, length us, event | category | flops | bytes accessed | tf_op | source)
XLA Modules:
  0.0 263.7 jit_solution(2767742694268110489)
XLA Ops:
  6.5 1.2 convert_reduce_fusion
  7.8 1.2 fusion.29
  9.0 1.2 fusion.31
  10.2 2.8 %stack.2 = bf16[16,128,1280]{2,1,0:T(8,128)(2,1)} broadcast(bf16[128,1280]{1,0:T(8,128)(2,1)S(1)} %fusion.31), dimensions={1,2} | broadcast | bytes 5570560 | tf_op jit(solution)/shard_map/stack | solution.py:37
  13.1 7.2 %all-to-all-start = ((bf16[16,128,1280]{2,1,0:T(8,128)(2,1)}), bf16[16,128,1280]{2,1,0:T(8,128)(2,1)}, u32[]{:S(2)}, u32[]{:S(2)}) async-start(bf16[16,128,1280]{2,1,0:T(8,128)(2,1)} %stack.2), calls=%async_computation | async-start | bytes 10485760 | tf_op jit(solution)/shard_map/all_to_all | solution.py:36
  20.3 0.0 all-gather.3.cloned.1.call-start
  20.3 87.8 %all_gather.9 = bf16[320,1280]{1,0:T(8,128)(2,1)} all-gather(bf16[80,1280]{1,0:T(8,128)(2,1)S(1)} %copy-done.4), channel_id=1, replica_groups=mesh['dp'=32,'seq_0'=4,'seq_1'=4] {'seq_1'}, dimensions={0}, use_global_device_ids=true | all-gather | bytes 1024000 | tf_op jit(solution)/shard_map/all_gather | solution.py:16
  108.2 0.0 all-gather.3.cloned.1.call-update
  108.2 0.0 copy-start.3
  108.2 4.2 %convolution_convert_fusion = bf16[2048,240]{0,1:T(8,128)(2,1)S(1)} fusion(bf16[2048,1280]{1,0:T(8,128)(2,1)} %bitcast.8, bf16[1280,240]{0,1:T(8,128)(2,1)} %param.11), kind=kOutput, calls=%fused_computation.19 | convolution fusion | flops 1258782720 | bytes 6840320 | tf_op jit(solution)/shard_map/dot_general | solution.py:34
  112.4 0.9 slice_bitcast_fusion
  113.3 0.2 copy-done.2
  113.5 25.1 %while.10 = (s32[]{:T(128)}, bf16[4,512,80]{1,2,0:T(8,128)(2,1)}, s32[4]{0:T(128)S(1)}, s32[2048]{0:T(1024)S(1)}, bf16[2048,1,3,80]{0,3,2,1:T(8,128)(2,1)}, /*in...) while((s32[]{:T(128)}, bf16[4,512,80]{1,2,0:T(8,128)(2,1)}, ...), condition=%wide.region_5.6_spmd, body=%wide.region_2.5_spmd.sunk | while | flops 352402432 | bytes 13447855 | solution.py:75
  113.5 0.6 dynamic_slice.12
  114.7 0.1 dynamic_slice.13
  114.8 1.9 fusion.46
  116.7 1.2 fusion.47
  117.9 1.9 fusion.48
  119.8 0.6 dynamic_slice.12
  120.9 0.1 dynamic_slice.13
  121.0 1.9 fusion.46
  122.9 1.2 fusion.47
  124.2 1.9 fusion.48
  126.0 0.6 dynamic_slice.12
  127.2 0.1 dynamic_slice.13
  127.3 1.9 fusion.46
  129.2 1.2 fusion.47
  130.5 1.9 fusion.48
  132.3 0.6 dynamic_slice.12
  133.5 0.1 dynamic_slice.13
  133.6 1.9 fusion.46
  135.5 1.2 fusion.47
  136.7 1.9 fusion.48
  138.6 1.2 copy.15
  139.9 0.8 all_to_all.32
  140.7 1.8 copy.16
  142.5 5.2 %all-to-all-start.1 = ((bf16[16,128,80]{1,2,0:T(8,128)(2,1)}), bf16[16,128,80]{1,2,0:T(8,128)(2,1)S(1)}, u32[]{:S(2)}, u32[]{:S(2)}) async-start(bf16[16,128,80]{1,2,0:T(8,128)(2,1)} %copy.16), calls=%async_computation.1 | async-start | bytes 655360 | tf_op jit(solution)/shard_map/all_to_all | solution.py:78
  147.7 0.0 all-gather.5.cloned.1.call-start
  147.8 14.7 %all-gather.3.cloned.1.call-done = bf16[1280,1280]{1,0:T(8,128)(2,1)} async-done(((bf16[320,1280]{1,0:T(8,128)(2,1)}), bf16[1280,1280]{1,0:T(8,128)(2,1)}) %all-gather.3.cloned.1.call-update) | async-done | bytes 3276816 | tf_op jit(solution)/shard_map/all_gather | solution.py:16
  162.5 2.6 %fusion.32 = (f32[128]{0:T(128)S(1)}, f32[128,1280]{1,0:T(8,128)S(1)}) fusion(bf16[128,1280]{0,1:T(8,128)(2,1)S(1)} %bitcast.65, bf16[1280,1280]{1,0:T(8,128)(2,1)} %all-gather.3.cloned.1.call-done, bf16[128,1280]{1,0:T(8,128)(2,1)S(1)} %copy-done.1), kind=kOutput, calls=%fused_computation.37 | convolution fusion | flops 419921792 | bytes 4588032 | tf_op jit(solution)/shard_map/dot_general | solution.py:79
  165.1 0.2 multiply_reduce_fusion
  165.4 0.2 multiply_convert_fusion
  165.5 0.9 reshape.83
  166.5 0.0 all-gather.5.cloned.1.call-update
  166.5 71.9 %all-gather.5.cloned.1.call-done = bf16[512,5120]{1,0:T(8,128)(2,1)} async-done(((bf16[32,5120]{1,0:T(8,128)(2,1)}), bf16[512,5120]{1,0:T(8,128)(2,1)}) %all-gather.5.cloned.1.call-update) | async-done | bytes 5242896 | tf_op jit(solution)/shard_map/all_gather | solution.py:86
  238.4 4.0 %convolution_convert_fusion.1 = bf16[512,256]{1,0:T(8,128)(2,1)S(1)} fusion(bf16[512,5120]{1,0:T(8,128)(2,1)} %all-gather.5.cloned.1.call-done, bf16[5120,256]{1,0:T(8,128)(2,1)S(1)} %copy-done), kind=kOutput, calls=%fused_computation.21 | convolution fusion | flops 1342308352 | bytes 8126464 | tf_op jit(solution)/shard_map/dot_general | solution.py:85
  242.4 13.7 %all_to_all.43 = bf16[16,32,256]{2,1,0:T(8,128)(2,1)S(1)} all-to-all(bf16[16,32,256]{2,1,0:T(8,128)(2,1)S(1)} %bitcast.69), channel_id=1, replica_groups=mesh['dp'=32,'seq_0'=4,'seq_1'=4] {'seq_0','seq_1'}, dimensions={0} | all-to-all | bytes 524288 | tf_op jit(solution)/shard_map/all_to_all | solution.py:88
  256.2 0.7 copy.18
  (18 shorter events, 0.1 us)
Async XLA Ops:
  6.5 231.9 %copy-start = (bf16[5120,256]{1,0:T(8,128)(2,1)S(1)}, bf16[5120,256]{1,0:T(8,128)(2,1)}, u32[]{:S(2)}) copy-start(bf16[5120,256]{1,0:T(8,128)(2,1)} %param.13) | copy-start | bytes 7864324
  13.1 7.3 %copy-start.4 = (bf16[80,1280]{1,0:T(8,128)(2,1)S(1)}, bf16[80,1280]{1,0:T(8,128)(2,1)}, u32[]{:S(2)}) copy-start(bf16[80,1280]{1,0:T(8,128)(2,1)} %param.12) | copy-start | bytes 614404
  13.1 95.2 %all-to-all-start = ((bf16[16,128,1280]{2,1,0:T(8,128)(2,1)}), bf16[16,128,1280]{2,1,0:T(8,128)(2,1)}, u32[]{:S(2)}, u32[]{:S(2)}) async-start(bf16[16,128,1280]{2,1,0:T(8,128)(2,1)} %stack.2), calls=%async_computation | async-start | bytes 10485760 | tf_op jit(solution)/shard_map/all_to_all | solution.py:36
  20.3 142.2 %all-gather.3.cloned.1.call-start = ((), (), s32[]{:S(2)}) async-start(), calls=%async_computation.3 | async-start | bytes 4096000 | tf_op jit(solution)/shard_map/all_gather | solution.py:16
  108.2 5.3 %copy-start.3 = (s32[2048]{0:T(1024)S(1)}, s32[2048]{0:T(1024)}, u32[]{:S(2)}) copy-start(s32[2048]{0:T(1024)} %param.10) | copy-start | bytes 24580
  112.4 1.1 copy-start.2
  113.5 49.0 %copy-start.1 = (bf16[128,1280]{1,0:T(8,128)(2,1)S(1)}, bf16[128,1280]{1,0:T(8,128)(2,1)}, u32[]{:S(2)}) copy-start(bf16[128,1280]{1,0:T(8,128)(2,1)} %param.9) | copy-start | bytes 983044
  138.6 26.7 %copy-start.5 = (f32[1280]{0:T(1024)S(1)}, f32[1280]{0:T(1024)}, u32[]{:S(2)}) copy-start(f32[1280]{0:T(1024)} %param.15) | copy-start | bytes 15364
  142.5 20.0 %all-to-all-start.1 = ((bf16[16,128,80]{1,2,0:T(8,128)(2,1)}), bf16[16,128,80]{1,2,0:T(8,128)(2,1)S(1)}, u32[]{:S(2)}, u32[]{:S(2)}) async-start(bf16[16,128,80]{1,2,0:T(8,128)(2,1)} %copy.16), calls=%async_computation.1 | async-start | bytes 655360 | tf_op jit(solution)/shard_map/all_to_all | solution.py:78
  147.7 90.7 %all-gather.5.cloned.1.call-start = ((), (), s32[]{:S(2)}) async-start(), calls=%async_computation.4 | async-start | bytes 5570560 | tf_op jit(solution)/shard_map/all_gather | solution.py:86
Sparse Core Ops, SparseCore 0:
  108.3 54.0 all-gather.2
  166.6 71.7 all-gather.4
